TPU v7x, 32 devices: a whole 2x2x4 slice. The times are simulated.
32 devices in a mesh: pair: 8 (over z, y), aux: 4 (over x, core).
Axes of the slice: x: 2, y: 2, z: 4, core: 2. Of those that a mesh axis runs over, the one named last changes fastest.
Arguments:
- pair_factors: bfloat16 [16384, 16384], P('pair', 'aux'), may hold values from -0.077339804 to 0.077339804
- pair_weights: float32 [16384], P('pair'), may hold values from 0.08 to 0.8
- probes: float32 [16384, 64], P('aux'), may hold values from -12 to 12
Outputs:
- last_vectors: float32 [16384, 64], P('aux', 'pair')
- moments: float32 [9], replicated
- energy: float32 [1], replicated
All inputs are finite; a program needn't handle non-finite values.
Results may differ from a plain program's by a relative error of at most 0.019.
Values may be sent and summed in bfloat16 or wider, within the bound.
No kernel may reach another device: no remote copies, remote signals or barrier semaphores. Data moves between devices by JAX's collectives and lax.ppermute only.
A program may use at most 64 MiB of HBM per device.

v0:
```python
import jax
import jax.numpy as jnp
import numpy as np
from jax import lax
from jax.sharding import PartitionSpec as P

ITERS = 8
spread = 5.0


def cheb_coefficients(order_count):
    node_count = 64
    angles = (np.arange(node_count) + 0.5) * np.pi / node_count
    samples = np.log(1.0 + spread * (np.cos(angles) + 1.0) / 2.0)
    values = [
        2.0 / node_count * np.sum(samples * np.cos(degree * angles))
        for degree in range(order_count)
    ]
    values[0] = values[0] / 2.0
    return np.array(values)


def per_device(pair_factors, pair_weights, probes):
    probe_total = probes.shape[1]
    divisor = probe_total * probes.shape[0] * lax.axis_size("aux")
    share = probe_total // lax.axis_size("pair")
    start = lax.axis_index("pair") * share
    own_probes = lax.dynamic_slice_in_dim(probes, start, share, 1)
    partials = [jnp.sum(own_probes * own_probes)]
    previous = probes
    current = probes
    for degree in range(ITERS):
        rows = jnp.dot(
            pair_factors, current.astype(jnp.bfloat16), preferred_element_type=jnp.float32
        )
        rows = lax.psum(rows, "aux")
        scaled = (pair_weights[:, None] * rows).astype(jnp.bfloat16)
        image = lax.psum(
            lax.dot_general(
                pair_factors, scaled, (((0,), (0,)), ((), ())), preferred_element_type=jnp.float32
            ),
            "pair",
        )
        mapped = 2.0 / spread * image - current
        following = mapped if degree == 0 else 2.0 * mapped - previous
        previous, current = (current, following)
        own_share = lax.dynamic_slice_in_dim(current, start, share, 1)
        partials.append(jnp.sum(own_probes * own_share))
    own_share = lax.dynamic_slice_in_dim(current, start, share, 1)
    totals = lax.psum(jnp.stack(partials), ("pair", "aux"))
    moments = totals / divisor
    coefficients = jnp.asarray(cheb_coefficients(ITERS + 1)).astype(moments.dtype)
    energy = jnp.sum(coefficients * moments).reshape(1)
    return (own_share, moments, energy)


def solution(mesh):
    placed = (P("pair", "aux"), P("pair"), P("aux", None))
    return jax.shard_map(
        per_device,
        mesh=mesh,
        in_specs=placed,
        out_specs=(P("aux", "pair"), P(), P()),
        check_vma=False,
    )
```

profile of v0, /device:TPU:0, one launch (start us, length us, event | category | flops | bytes accessed | tf_op | source)
XLA Modules:
  0.0 1159.6 jit_solution(14180925838934480082)
XLA Ops:
  7.2 11.6 fusion.7
  18.8 39.1 %all-reduce.17.cloned.1.call-done = f32[2048,64]{1,0:T(8,128)} async-done(((f32[2048,64]{1,0:T(8,128)}), f32[2048,64]{1,0:T(8,128)}) %all-reduce.17.cloned.1.call-update) | async-done | bytes 524304 | tf_op jit(solution)/shard_map/psum | solution.py:36
  58.0 10.3 convolution_bitcast_fusion.7
  68.3 78.9 %all-reduce.19.cloned.1.call-done = f32[4096,64]{0,1:T(8,128)} async-done(((f32[4096,64]{0,1:T(8,128)}), f32[4096,64]{0,1:T(8,128)}) %all-reduce.19.cloned.1.call-update) | async-done | bytes 1048592 | tf_op jit(solution)/shard_map/psum | solution.py:38
  148.6 9.2 convolution_bitcast_fusion.14
  158.4 35.5 %all-reduce.21.cloned.1.call-done = f32[2048,64]{1,0:T(8,128)} async-done(((f32[2048,64]{1,0:T(8,128)}), f32[2048,64]{1,0:T(8,128)}) %all-reduce.21.cloned.1.call-update) | async-done | bytes 524304 | tf_op jit(solution)/shard_map/psum | solution.py:36
  193.8 10.3 convolution_bitcast_fusion.6
  204.2 79.0 %all-reduce.23.cloned.1.call-done = f32[4096,64]{0,1:T(8,128)} async-done(((f32[4096,64]{0,1:T(8,128)}), f32[4096,64]{0,1:T(8,128)}) %all-reduce.23.cloned.1.call-update) | async-done | bytes 1048592 | tf_op jit(solution)/shard_map/psum | solution.py:38
  284.6 9.2 convolution_bitcast_fusion.13
  293.8 36.0 %all-reduce.25.cloned.1.call-done = f32[2048,64]{1,0:T(8,128)} async-done(((f32[2048,64]{1,0:T(8,128)}), f32[2048,64]{1,0:T(8,128)}) %all-reduce.25.cloned.1.call-update) | async-done | bytes 524304 | tf_op jit(solution)/shard_map/psum | solution.py:36
  329.8 10.3 convolution_bitcast_fusion.5
  340.2 79.0 %all-reduce.27.cloned.1.call-done = f32[4096,64]{0,1:T(8,128)} async-done(((f32[4096,64]{0,1:T(8,128)}), f32[4096,64]{0,1:T(8,128)}) %all-reduce.27.cloned.1.call-update) | async-done | bytes 1048592 | tf_op jit(solution)/shard_map/psum | solution.py:38
  420.6 9.2 convolution_bitcast_fusion.12
  430.0 35.8 %all-reduce.29.cloned.1.call-done = f32[2048,64]{1,0:T(8,128)} async-done(((f32[2048,64]{1,0:T(8,128)}), f32[2048,64]{1,0:T(8,128)}) %all-reduce.29.cloned.1.call-update) | async-done | bytes 524304 | tf_op jit(solution)/shard_map/psum | solution.py:36
  465.8 10.3 convolution_bitcast_fusion.4
  476.2 79.0 %all-reduce.31.cloned.1.call-done = f32[4096,64]{0,1:T(8,128)} async-done(((f32[4096,64]{0,1:T(8,128)}), f32[4096,64]{0,1:T(8,128)}) %all-reduce.31.cloned.1.call-update) | async-done | bytes 1048592 | tf_op jit(solution)/shard_map/psum | solution.py:38
  557.5 9.1 convolution_bitcast_fusion.11
  566.7 36.0 %all-reduce.33.cloned.1.call-done = f32[2048,64]{1,0:T(8,128)} async-done(((f32[2048,64]{1,0:T(8,128)}), f32[2048,64]{1,0:T(8,128)}) %all-reduce.33.cloned.1.call-update) | async-done | bytes 524304 | tf_op jit(solution)/shard_map/psum | solution.py:36
  602.7 10.2 convolution_bitcast_fusion.3
  613.0 78.9 %all-reduce.35.cloned.1.call-done = f32[4096,64]{0,1:T(8,128)} async-done(((f32[4096,64]{0,1:T(8,128)}), f32[4096,64]{0,1:T(8,128)}) %all-reduce.35.cloned.1.call-update) | async-done | bytes 1048592 | tf_op jit(solution)/shard_map/psum | solution.py:38
  694.7 9.1 convolution_bitcast_fusion.10
  704.0 35.8 %all-reduce.37.cloned.1.call-done = f32[2048,64]{1,0:T(8,128)} async-done(((f32[2048,64]{1,0:T(8,128)}), f32[2048,64]{1,0:T(8,128)}) %all-reduce.37.cloned.1.call-update) | async-done | bytes 524304 | tf_op jit(solution)/shard_map/psum | solution.py:36
  739.8 10.2 convolution_bitcast_fusion.2
  750.2 78.8 %all-reduce.39.cloned.1.call-done = f32[4096,64]{0,1:T(8,128)} async-done(((f32[4096,64]{0,1:T(8,128)}), f32[4096,64]{0,1:T(8,128)}) %all-reduce.39.cloned.1.call-update) | async-done | bytes 1048592 | tf_op jit(solution)/shard_map/psum | solution.py:38
  841.2 36.0 %all-reduce.41.cloned.1.call-done = f32[2048,64]{1,0:T(8,128)} async-done(((f32[2048,64]{1,0:T(8,128)}), f32[2048,64]{1,0:T(8,128)}) %all-reduce.41.cloned.1.call-update) | async-done | bytes 524304 | tf_op jit(solution)/shard_map/psum | solution.py:36
  877.2 10.2 convolution_bitcast_fusion.1
  887.5 78.9 %all-reduce.43.cloned.1.call-done = f32[4096,64]{0,1:T(8,128)} async-done(((f32[4096,64]{0,1:T(8,128)}), f32[4096,64]{0,1:T(8,128)}) %all-reduce.43.cloned.1.call-update) | async-done | bytes 1048592 | tf_op jit(solution)/shard_map/psum | solution.py:38
  969.4 9.1 convolution_bitcast_fusion.8
  978.8 35.7 %all-reduce.45.cloned.1.call-done = f32[2048,64]{1,0:T(8,128)} async-done(((f32[2048,64]{1,0:T(8,128)}), f32[2048,64]{1,0:T(8,128)}) %all-reduce.45.cloned.1.call-update) | async-done | bytes 524304 | tf_op jit(solution)/shard_map/psum | solution.py:36
  1014.6 10.3 convolution_bitcast_fusion
  1024.9 78.9 %all-reduce.47.cloned.1.call-done = f32[4096,64]{0,1:T(8,128)} async-done(((f32[4096,64]{0,1:T(8,128)}), f32[4096,64]{0,1:T(8,128)}) %all-reduce.47.cloned.1.call-update) | async-done | bytes 1048592 | tf_op jit(solution)/shard_map/psum | solution.py:38
  1112.1 39.5 %psum.135 = f32[9]{0:T(128)S(1)} all-reduce(f32[9]{0:T(128)S(1)} %stack.39), channel_id=1, replica_groups=mesh['pair'=8,'aux'=4] {'pair','aux'}, use_global_device_ids=true, to_apply=%region_25.0 | all-reduce | flops 9 | bytes 72 | tf_op jit(solution)/shard_map/psum | solution.py:50
  (57 shorter events, 35.9 us)
Async XLA Ops:
  7.2 50.8 %copy-start.5 = (f32[2048]{0:T(1024)S(1)}, f32[2048]{0:T(1024)}, u32[]{:S(2)}) copy-start(f32[2048]{0:T(1024)} %param.5) | copy-start | bytes 24580
  7.2 50.8 %all-reduce.17.cloned.1.call-start = ((), (), s32[]{:S(2)}) async-start(), calls=%async_computation | async-start | bytes 2097152 | tf_op jit(solution)/shard_map/psum | solution.py:36
  18.8 128.5 %copy-start.4 = (f32[4096,64]{0,1:T(8,128)S(1)}, f32[4096,64]{0,1:T(8,128)}, u32[]{:S(2)}) copy-start(f32[4096,64]{0,1:T(8,128)} %param.6) | copy-start | bytes 3145732
  18.8 128.4 %all-reduce.19.cloned.1.call-start = ((), (), s32[]{:S(2)}) async-start(), calls=%async_computation.1 | async-start | bytes 2097152 | tf_op jit(solution)/shard_map/psum | solution.py:38
  68.3 125.5 %all-reduce.21.cloned.1.call-start = ((), (), s32[]{:S(2)}) async-start(), calls=%async_computation.2 | async-start | bytes 2097152 | tf_op jit(solution)/shard_map/psum | solution.py:36
  157.8 125.4 %all-reduce.23.cloned.1.call-start = ((), (), s32[]{:S(2)}) async-start(), calls=%async_computation.3 | async-start | bytes 2097152 | tf_op jit(solution)/shard_map/psum | solution.py:38
  204.1 125.7 %all-reduce.25.cloned.1.call-start = ((), (), s32[]{:S(2)}) async-start(), calls=%async_computation.4 | async-start | bytes 2097152 | tf_op jit(solution)/shard_map/psum | solution.py:36
  293.8 125.4 %all-reduce.27.cloned.1.call-start = ((), (), s32[]{:S(2)}) async-start(), calls=%async_computation.5 | async-start | bytes 2097152 | tf_op jit(solution)/shard_map/psum | solution.py:38
  340.1 125.7 %all-reduce.29.cloned.1.call-start = ((), (), s32[]{:S(2)}) async-start(), calls=%async_computation.6 | async-start | bytes 2097152 | tf_op jit(solution)/shard_map/psum | solution.py:36
  429.8 125.4 %all-reduce.31.cloned.1.call-start = ((), (), s32[]{:S(2)}) async-start(), calls=%async_computation.7 | async-start | bytes 2097152 | tf_op jit(solution)/shard_map/psum | solution.py:38
  476.1 126.6 %all-reduce.33.cloned.1.call-start = ((), (), s32[]{:S(2)}) async-start(), calls=%async_computation.8 | async-start | bytes 2097152 | tf_op jit(solution)/shard_map/psum | solution.py:36
  556.6 1.0 copy-start
  566.7 125.2 %all-reduce.35.cloned.1.call-start = ((), (), s32[]{:S(2)}) async-start(), calls=%async_computation.9 | async-start | bytes 2097152 | tf_op jit(solution)/shard_map/psum | solution.py:38
  613.0 126.8 %all-reduce.37.cloned.1.call-start = ((), (), s32[]{:S(2)}) async-start(), calls=%async_computation.10 | async-start | bytes 2097152 | tf_op jit(solution)/shard_map/psum | solution.py:36
  693.6 1.0 copy-start.1
  703.8 125.2 %all-reduce.39.cloned.1.call-start = ((), (), s32[]{:S(2)}) async-start(), calls=%async_computation.11 | async-start | bytes 2097152 | tf_op jit(solution)/shard_map/psum | solution.py:38
  750.1 127.0 %all-reduce.41.cloned.1.call-start = ((), (), s32[]{:S(2)}) async-start(), calls=%async_computation.12 | async-start | bytes 2097152 | tf_op jit(solution)/shard_map/psum | solution.py:36
  831.0 1.0 copy-start.2
  841.1 125.2 %all-reduce.43.cloned.1.call-start = ((), (), s32[]{:S(2)}) async-start(), calls=%async_computation.13 | async-start | bytes 2097152 | tf_op jit(solution)/shard_map/psum | solution.py:38
  887.4 127.1 %all-reduce.45.cloned.1.call-start = ((), (), s32[]{:S(2)}) async-start(), calls=%async_computation.14 | async-start | bytes 2097152 | tf_op jit(solution)/shard_map/psum | solution.py:36
  968.4 1.0 copy-start.3
  978.5 173.2 %copy-start.6 = (f32[9]{0:T(128)S(1)}, f32[9]{0:T(128)}, u32[]{:S(2)}) copy-start(f32[9]{0:T(128)} %constant.23.clone) | copy-start | bytes 112
  978.5 125.3 %all-reduce.47.cloned.1.call-start = ((), (), s32[]{:S(2)}) async-start(), calls=%async_computation.15 | async-start | bytes 2097152 | tf_op jit(solution)/shard_map/psum | solution.py:38
Sparse Core Ops, SparseCore 0:
  18.9 39.0 all-reduce.16
  68.4 78.7 all-reduce.18
  157.9 35.8 all-reduce.20
  204.3 78.8 all-reduce.22
  293.9 35.8 all-reduce.24
  340.3 78.8 all-reduce.26
  429.9 35.8 all-reduce.28
  476.2 78.8 all-reduce.30
  566.8 35.8 all-reduce.32
  613.1 78.7 all-reduce.34
  703.9 35.8 all-reduce.36
  750.2 78.7 all-reduce.38
  841.2 35.8 all-reduce.40
  887.5 78.7 all-reduce.42
  978.6 35.8 all-reduce.44
  1025.0 78.7 all-reduce.46
where the time goes:
time: 1170 us; the launch traced here: 1160 us
  waiting for transfers between devices  922 us (79%)
  matrix products  158 us (14%)
  blocking collectives  39.5 us (3%)
  other arithmetic  15.1 us (1%)
  between operations  14.3 us (1%)
    psum x8, waiting for transfers between devices, per_device(): lax.psum(lax.dot_general(pair_factors, scaled, (((0,), (0,)), ((), ())),...  631 us
    psum x8, waiting for transfers between devices, per_device(): rows = lax.psum(rows, 'aux')  290 us
    dot_general x8, matrix products, per_device(): lax.dot_general(pair_factors, scaled, (((0,), (0,)), ((), ())), preferred...  82.2 us
    dot_general x8, matrix products, per_device(): jnp.dot(pair_factors, current.astype(jnp.bfloat16), preferred_element_typ...  75.4 us
    psum x1, blocking collectives, per_device(): totals = lax.psum(jnp.stack(partials), ('pair', 'aux'))  39.5 us
  transfers between devices with their start and end apart: 16, of which 16 were waited for; matrix products, arithmetic and copies ran while one was open for 0% of the time, Pallas kernels for 0%

commit v1 on v0

--- a/solution.py
+++ b/solution.py
@@ -33,7 +33,15 @@
         rows = jnp.dot(
             pair_factors, current.astype(jnp.bfloat16), preferred_element_type=jnp.float32
         )
-        rows = lax.psum(rows, "aux")
+        kept_arr = rows
+        n_chips = lax.axis_size("aux")
+        for nth in [
+            [(dev_i, dev_i ^ d) for dev_i in range(n_chips)]
+            for d in (1, 2, 4, 8, 16)
+            if d < n_chips
+        ]:
+            kept_arr = kept_arr + lax.ppermute(kept_arr, axis_name="aux", perm=nth)
+        rows = kept_arr
         scaled = (pair_weights[:, None] * rows).astype(jnp.bfloat16)
         image = lax.psum(
             lax.dot_general(

time: 1170 us -> 1010 us (0.86)
  waiting for transfers between devices: 922 us -> 740 us
  starting transfers between devices: 1.83 us -> 16.9 us
    psum x8 -> x0, waiting for transfers between devices: 290 us -> none  [per_device(): rows = lax.psum(rows, 'aux')]
    ppermute x0 -> x16, waiting for transfers between devices: none -> 116 us  [per_device(): kept_arr = kept_arr + lax.ppermute(kept_arr, axis_name='aux', perm=nth)]
    dot_general x8, matrix products: 75.4 us -> 93.3 us  [per_device(): jnp.dot(pair_factors, current.astype(jnp.bfloat16), preferred_element_typ...]
    ppermute x0 -> x16, starting transfers between devices: none -> 14.3 us  [per_device(): kept_arr = kept_arr + lax.ppermute(kept_arr, axis_name='aux', perm=nth)]
  transfers between devices with their start and end apart: 16 -> 24, of which waited for: 16 -> 24; matrix products, arithmetic and copies ran while one was open for 0% -> 0% of each run, Pallas kernels for 0% -> 0%
where the time goes in v1:
time: 1010 us
  waiting for transfers between devices  740 us (73%)
  matrix products  166 us (16%)
  blocking collectives  39.5 us (4%)
  other arithmetic  24.9 us (2%)
  starting transfers between devices  16.9 us (2%)
  between operations  14.4 us (1%)
    psum x8, waiting for transfers between devices, per_device(): lax.psum(lax.dot_general(pair_factors, scaled, (((0,), (0,)), ((), ())),...  624 us
    ppermute x16, waiting for transfers between devices, per_device(): kept_arr = kept_arr + lax.ppermute(kept_arr, axis_name='aux', perm=nth)  116 us
    dot_general x8, matrix products, per_device(): jnp.dot(pair_factors, current.astype(jnp.bfloat16), preferred_element_typ...  93.3 us
    dot_general x8, matrix products, per_device(): lax.dot_general(pair_factors, scaled, (((0,), (0,)), ((), ())), preferred...  72.9 us
    psum x1, blocking collectives, per_device(): totals = lax.psum(jnp.stack(partials), ('pair', 'aux'))  39.5 us
  transfers between devices with their start and end apart: 24, of which 24 were waited for; matrix products, arithmetic and copies ran while one was open for 0% of the time, Pallas kernels for 0%

profile of v1, /device:TPU:0, one launch (start us, length us, event | category | flops | bytes accessed | tf_op | source)
XLA Modules:
  0.0 1007.4 jit_solution(15265576410393871616)
XLA Ops:
  7.2 11.3 %fusion.7 = f32[2048,64]{0,1:T(8,128)S(1)} fusion(bf16[2048,4096]{1,0:T(8,128)(2,1)} %param.4, f32[4096,64]{0,1:T(8,128)} %param.6), kind=kOutput, calls=%fused_computation.37 | convolution fusion | flops 1074003968 | bytes 18350080 | tf_op jit(solution)/shard_map/dot_general | solution.py:33
  23.6 12.2 %collective-permute-done.1 = f32[2048,64]{0,1:T(8,128)S(1)} collective-permute-done((f32[2048,64]{0,1:T(8,128)S(1)}, f32[2048,64]{0,1:T(8,128)S(1)}, u32[]{:S(2)}, u32[]{:S(2)}) %collective-permute-start.1) | collective-permute-done | bytes 524320 | tf_op jit(solution)/shard_map/ppermute | solution.py:43
  40.6 79.4 %all-reduce.9.cloned.1.call-done = f32[4096,64]{0,1:T(8,128)} async-done(((f32[4096,64]{0,1:T(8,128)}), f32[4096,64]{0,1:T(8,128)}) %all-reduce.9.cloned.1.call-update) | async-done | bytes 1048592 | tf_op jit(solution)/shard_map/psum | solution.py:46
  121.4 11.0 %convolution_bitcast_fusion.14 = f32[2048,64]{0,1:T(8,128)S(1)} fusion(bf16[2048,4096]{1,0:T(8,128)(2,1)} %param.4, f32[4096,64]{0,1:T(8,128)S(1)} %multiply_subtract_fusion.6), kind=kOutput, calls=%fused_computation.14 | convolution fusion | flops 1074003968 | bytes 18350080 | tf_op jit(solution)/shard_map/dot_general | solution.py:33
  135.9 12.5 %collective-permute-done.3 = f32[2048,64]{0,1:T(8,128)S(1)} collective-permute-done((f32[2048,64]{0,1:T(8,128)S(1)}, f32[2048,64]{0,1:T(8,128)S(1)}, u32[]{:S(2)}, u32[]{:S(2)}) %collective-permute-start.3) | collective-permute-done | bytes 524320 | tf_op jit(solution)/shard_map/ppermute | solution.py:43
  148.4 9.8 convolution_bitcast_fusion.6
  158.5 77.9 %all-reduce.11.cloned.1.call-done = f32[4096,64]{0,1:T(8,128)} async-done(((f32[4096,64]{0,1:T(8,128)}), f32[4096,64]{0,1:T(8,128)}) %all-reduce.11.cloned.1.call-update) | async-done | bytes 1048592 | tf_op jit(solution)/shard_map/psum | solution.py:46
  237.8 11.0 %convolution_bitcast_fusion.13 = f32[2048,64]{0,1:T(8,128)S(1)} fusion(bf16[2048,4096]{1,0:T(8,128)(2,1)} %param.4, f32[4096,64]{0,1:T(8,128)S(1)} %multiply_subtract_fusion.5), kind=kOutput, calls=%fused_computation.13 | convolution fusion | flops 1074003968 | bytes 18350080 | tf_op jit(solution)/shard_map/dot_general | solution.py:33
  252.3 12.5 %collective-permute-done.5 = f32[2048,64]{0,1:T(8,128)S(1)} collective-permute-done((f32[2048,64]{0,1:T(8,128)S(1)}, f32[2048,64]{0,1:T(8,128)S(1)}, u32[]{:S(2)}, u32[]{:S(2)}) %collective-permute-start.5) | collective-permute-done | bytes 524320 | tf_op jit(solution)/shard_map/ppermute | solution.py:43
  264.8 9.8 convolution_bitcast_fusion.5
  275.0 77.8 %all-reduce.13.cloned.1.call-done = f32[4096,64]{0,1:T(8,128)} async-done(((f32[4096,64]{0,1:T(8,128)}), f32[4096,64]{0,1:T(8,128)}) %all-reduce.13.cloned.1.call-update) | async-done | bytes 1048592 | tf_op jit(solution)/shard_map/psum | solution.py:46
  354.2 11.7 %convolution_bitcast_fusion.12 = f32[2048,64]{0,1:T(8,128)} fusion(bf16[2048,4096]{1,0:T(8,128)(2,1)} %param.4, f32[4096,64]{0,1:T(8,128)S(1)} %multiply_subtract_fusion.4), kind=kOutput, calls=%fused_computation.12 | convolution fusion | flops 1074003968 | bytes 18350080 | tf_op jit(solution)/shard_map/dot_general | solution.py:33
  370.7 12.5 %collective-permute-done.7 = f32[2048,64]{0,1:T(8,128)S(1)} collective-permute-done((f32[2048,64]{0,1:T(8,128)S(1)}, f32[2048,64]{0,1:T(8,128)S(1)}, u32[]{:S(2)}, u32[]{:S(2)}) %collective-permute-start.7) | collective-permute-done | bytes 524320 | tf_op jit(solution)/shard_map/ppermute | solution.py:43
  383.2 9.8 convolution_bitcast_fusion.4
  393.3 77.8 %all-reduce.15.cloned.1.call-done = f32[4096,64]{0,1:T(8,128)} async-done(((f32[4096,64]{0,1:T(8,128)}), f32[4096,64]{0,1:T(8,128)}) %all-reduce.15.cloned.1.call-update) | async-done | bytes 1048592 | tf_op jit(solution)/shard_map/psum | solution.py:46
  473.5 12.1 %convolution_bitcast_fusion.11 = f32[2048,64]{0,1:T(8,128)} fusion(bf16[2048,4096]{1,0:T(8,128)(2,1)} %param.4, f32[4096,64]{0,1:T(8,128)} %multiply_subtract_fusion.3), kind=kOutput, calls=%fused_computation.11 | convolution fusion | flops 1074003968 | bytes 18350080 | tf_op jit(solution)/shard_map/dot_general | solution.py:33
  490.4 12.5 %collective-permute-done.9 = f32[2048,64]{0,1:T(8,128)S(1)} collective-permute-done((f32[2048,64]{0,1:T(8,128)S(1)}, f32[2048,64]{0,1:T(8,128)S(1)}, u32[]{:S(2)}, u32[]{:S(2)}) %collective-permute-start.9) | collective-permute-done | bytes 524320 | tf_op jit(solution)/shard_map/ppermute | solution.py:43
  502.9 9.9 convolution_bitcast_fusion.3
  513.1 77.7 %all-reduce.17.cloned.1.call-done = f32[4096,64]{0,1:T(8,128)} async-done(((f32[4096,64]{0,1:T(8,128)}), f32[4096,64]{0,1:T(8,128)}) %all-reduce.17.cloned.1.call-update) | async-done | bytes 1048592 | tf_op jit(solution)/shard_map/psum | solution.py:46
  593.6 12.1 %convolution_bitcast_fusion.10 = f32[2048,64]{0,1:T(8,128)} fusion(bf16[2048,4096]{1,0:T(8,128)(2,1)} %param.4, f32[4096,64]{0,1:T(8,128)} %multiply_subtract_fusion.2), kind=kOutput, calls=%fused_computation.10 | convolution fusion | flops 1074003968 | bytes 18350080 | tf_op jit(solution)/shard_map/dot_general | solution.py:33
  610.4 12.5 %collective-permute-done.11 = f32[2048,64]{0,1:T(8,128)S(1)} collective-permute-done((f32[2048,64]{0,1:T(8,128)S(1)}, f32[2048,64]{0,1:T(8,128)S(1)}, u32[]{:S(2)}, u32[]{:S(2)}) %collective-permute-start.11) | collective-permute-done | bytes 524320 | tf_op jit(solution)/shard_map/ppermute | solution.py:43
  622.9 9.8 convolution_bitcast_fusion.2
  633.3 77.5 %all-reduce.19.cloned.1.call-done = f32[4096,64]{0,1:T(8,128)} async-done(((f32[4096,64]{0,1:T(8,128)}), f32[4096,64]{0,1:T(8,128)}) %all-reduce.19.cloned.1.call-update) | async-done | bytes 1048592 | tf_op jit(solution)/shard_map/psum | solution.py:46
  713.8 12.1 %convolution_bitcast_fusion.9 = f32[2048,64]{0,1:T(8,128)} fusion(bf16[2048,4096]{1,0:T(8,128)(2,1)} %param.4, f32[4096,64]{0,1:T(8,128)} %multiply_subtract_fusion.1), kind=kOutput, calls=%fused_computation.9 | convolution fusion | flops 1074003968 | bytes 18350080 | tf_op jit(solution)/shard_map/dot_general | solution.py:33
  730.7 12.5 %collective-permute-done.13 = f32[2048,64]{0,1:T(8,128)S(1)} collective-permute-done((f32[2048,64]{0,1:T(8,128)S(1)}, f32[2048,64]{0,1:T(8,128)S(1)}, u32[]{:S(2)}, u32[]{:S(2)}) %collective-permute-start.13) | collective-permute-done | bytes 524320 | tf_op jit(solution)/shard_map/ppermute | solution.py:43
  743.2 9.8 convolution_bitcast_fusion.1
  753.3 77.9 %all-reduce.21.cloned.1.call-done = f32[4096,64]{0,1:T(8,128)} async-done(((f32[4096,64]{0,1:T(8,128)}), f32[4096,64]{0,1:T(8,128)}) %all-reduce.21.cloned.1.call-update) | async-done | bytes 1048592 | tf_op jit(solution)/shard_map/psum | solution.py:46
  834.1 12.1 %convolution_bitcast_fusion.8 = f32[2048,64]{0,1:T(8,128)} fusion(bf16[2048,4096]{1,0:T(8,128)(2,1)} %param.4, f32[4096,64]{0,1:T(8,128)} %multiply_subtract_fusion), kind=kOutput, calls=%fused_computation.8 | convolution fusion | flops 1074003968 | bytes 18350080 | tf_op jit(solution)/shard_map/dot_general | solution.py:33
  851.0 12.5 %collective-permute-done.15 = f32[2048,64]{0,1:T(8,128)S(1)} collective-permute-done((f32[2048,64]{0,1:T(8,128)S(1)}, f32[2048,64]{0,1:T(8,128)S(1)}, u32[]{:S(2)}, u32[]{:S(2)}) %collective-permute-start.15) | collective-permute-done | bytes 524320 | tf_op jit(solution)/shard_map/ppermute | solution.py:43
  863.5 9.8 convolution_bitcast_fusion
  873.4 78.0 %all-reduce.23.cloned.1.call-done = f32[4096,64]{0,1:T(8,128)} async-done(((f32[4096,64]{0,1:T(8,128)}), f32[4096,64]{0,1:T(8,128)}) %all-reduce.23.cloned.1.call-update) | async-done | bytes 1048592 | tf_op jit(solution)/shard_map/psum | solution.py:46
  959.7 39.5 %psum.71 = f32[9]{0:T(128)S(1)} all-reduce(f32[9]{0:T(128)S(1)} %stack.39), channel_id=1, replica_groups=mesh['pair'=8,'aux'=4] {'pair','aux'}, use_global_device_ids=true, to_apply=%region_17.0 | all-reduce | flops 9 | bytes 72 | tf_op jit(solution)/shard_map/psum | solution.py:58
  (67 shorter events, 67.7 us)
Async XLA Ops:
  7.2 28.7 %copy-start.2 = (f32[2048]{0:T(1024)S(1)}, f32[2048]{0:T(1024)}, u32[]{:S(2)}) copy-start(f32[2048]{0:T(1024)} %param.5) | copy-start | bytes 24580
  7.2 112.9 %all-reduce.9.cloned.1.call-start = ((), (), s32[]{:S(2)}) async-start(), calls=%async_computation | async-start | bytes 2097152 | tf_op jit(solution)/shard_map/psum | solution.py:46
  7.2 28.6 %copy-start = (bf16[2048,4096]{1,0:T(8,128)(2,1)S(1)}, bf16[2048,4096]{1,0:T(8,128)(2,1)}, u32[]{:S(2)}) copy-start(bf16[2048,4096]{1,0:T(8,128)(2,1)} %param.4) | copy-start | bytes 50331652
  18.6 101.5 %copy-start.1 = (f32[4096,64]{0,1:T(8,128)S(1)}, f32[4096,64]{0,1:T(8,128)}, u32[]{:S(2)}) copy-start(f32[4096,64]{0,1:T(8,128)} %param.6) | copy-start | bytes 3145732
  18.6 2.1 collective-permute-start
  20.7 15.1 %collective-permute-start.1 = (f32[2048,64]{0,1:T(8,128)S(1)}, f32[2048,64]{0,1:T(8,128)S(1)}, u32[]{:S(2)}, u32[]{:S(2)}) collective-permute-start(f32[2048,64]{0,1:T(8,128)S(1)} %add.78), channel_id=1, source_target_pairs={{0,2},{1,3},{2,0},{3,1},{4,6},{5,7},{6,4},{7,5},{8,10},{9,11},{10,... | collective-permute-start | bytes 1572872 | tf_op jit(solution)/shard_map/ppermute | solution.py:43
  40.0 196.4 %all-reduce.11.cloned.1.call-start = ((), (), s32[]{:S(2)}) async-start(), calls=%async_computation.1 | async-start | bytes 2097152 | tf_op jit(solution)/shard_map/psum | solution.py:46
  132.4 2.0 collective-permute-start.2
  134.4 14.0 %collective-permute-start.3 = (f32[2048,64]{0,1:T(8,128)S(1)}, f32[2048,64]{0,1:T(8,128)S(1)}, u32[]{:S(2)}, u32[]{:S(2)}) collective-permute-start(f32[2048,64]{0,1:T(8,128)S(1)} %add.80), channel_id=1, source_target_pairs={{0,2},{1,3},{2,0},{3,1},{4,6},{5,7},{6,4},{7,5},{8,10},{9,11},{10,... | collective-permute-start | bytes 1572872 | tf_op jit(solution)/shard_map/ppermute | solution.py:43
  158.3 194.5 %all-reduce.13.cloned.1.call-start = ((), (), s32[]{:S(2)}) async-start(), calls=%async_computation.2 | async-start | bytes 2097152 | tf_op jit(solution)/shard_map/psum | solution.py:46
  248.8 2.0 collective-permute-start.4
  250.8 14.0 %collective-permute-start.5 = (f32[2048,64]{0,1:T(8,128)S(1)}, f32[2048,64]{0,1:T(8,128)S(1)}, u32[]{:S(2)}, u32[]{:S(2)}) collective-permute-start(f32[2048,64]{0,1:T(8,128)S(1)} %add.82), channel_id=1, source_target_pairs={{0,2},{1,3},{2,0},{3,1},{4,6},{5,7},{6,4},{7,5},{8,10},{9,11},{10,... | collective-permute-start | bytes 1572872 | tf_op jit(solution)/shard_map/ppermute | solution.py:43
  274.7 196.4 %all-reduce.15.cloned.1.call-start = ((), (), s32[]{:S(2)}) async-start(), calls=%async_computation.3 | async-start | bytes 2097152 | tf_op jit(solution)/shard_map/psum | solution.py:46
  365.9 2.1 collective-permute-start.6
  369.1 14.0 %collective-permute-start.7 = (f32[2048,64]{0,1:T(8,128)S(1)}, f32[2048,64]{0,1:T(8,128)S(1)}, u32[]{:S(2)}, u32[]{:S(2)}) collective-permute-start(f32[2048,64]{0,1:T(8,128)S(1)} %add.84), channel_id=1, source_target_pairs={{0,2},{1,3},{2,0},{3,1},{4,6},{5,7},{6,4},{7,5},{8,10},{9,11},{10,... | collective-permute-start | bytes 1572872 | tf_op jit(solution)/shard_map/ppermute | solution.py:43
  393.0 197.8 %all-reduce.17.cloned.1.call-start = ((), (), s32[]{:S(2)}) async-start(), calls=%async_computation.4 | async-start | bytes 2097152 | tf_op jit(solution)/shard_map/psum | solution.py:46
  485.6 2.1 collective-permute-start.8
  488.9 14.0 %collective-permute-start.9 = (f32[2048,64]{0,1:T(8,128)S(1)}, f32[2048,64]{0,1:T(8,128)S(1)}, u32[]{:S(2)}, u32[]{:S(2)}) collective-permute-start(f32[2048,64]{0,1:T(8,128)S(1)} %add.86), channel_id=1, source_target_pairs={{0,2},{1,3},{2,0},{3,1},{4,6},{5,7},{6,4},{7,5},{8,10},{9,11},{10,... | collective-permute-start | bytes 1572872 | tf_op jit(solution)/shard_map/ppermute | solution.py:43
  512.8 198.0 %all-reduce.19.cloned.1.call-start = ((), (), s32[]{:S(2)}) async-start(), calls=%async_computation.5 | async-start | bytes 2097152 | tf_op jit(solution)/shard_map/psum | solution.py:46
  605.6 2.1 collective-permute-start.10
  608.9 14.0 %collective-permute-start.11 = (f32[2048,64]{0,1:T(8,128)S(1)}, f32[2048,64]{0,1:T(8,128)S(1)}, u32[]{:S(2)}, u32[]{:S(2)}) collective-permute-start(f32[2048,64]{0,1:T(8,128)S(1)} %add.88), channel_id=1, source_target_pairs={{0,2},{1,3},{2,0},{3,1},{4,6},{5,7},{6,4},{7,5},{8,10},{9,11},{10,... | collective-permute-start | bytes 1572872 | tf_op jit(solution)/shard_map/ppermute | solution.py:43
  632.8 198.4 %all-reduce.21.cloned.1.call-start = ((), (), s32[]{:S(2)}) async-start(), calls=%async_computation.6 | async-start | bytes 2097152 | tf_op jit(solution)/shard_map/psum | solution.py:46
  725.9 2.1 collective-permute-start.12
  729.2 14.0 %collective-permute-start.13 = (f32[2048,64]{0,1:T(8,128)S(1)}, f32[2048,64]{0,1:T(8,128)S(1)}, u32[]{:S(2)}, u32[]{:S(2)}) collective-permute-start(f32[2048,64]{0,1:T(8,128)S(1)} %add.90), channel_id=1, source_target_pairs={{0,2},{1,3},{2,0},{3,1},{4,6},{5,7},{6,4},{7,5},{8,10},{9,11},{10,... | collective-permute-start | bytes 1572872 | tf_op jit(solution)/shard_map/ppermute | solution.py:43
  753.0 198.3 %all-reduce.23.cloned.1.call-start = ((), (), s32[]{:S(2)}) async-start(), calls=%async_computation.7 | async-start | bytes 2097152 | tf_op jit(solution)/shard_map/psum | solution.py:46
  846.2 153.0 %copy-start.3 = (f32[9]{0:T(128)S(1)}, f32[9]{0:T(128)}, u32[]{:S(2)}) copy-start(f32[9]{0:T(128)} %constant.23.clone) | copy-start | bytes 112
  846.2 2.1 collective-permute-start.14
  849.5 14.0 %collective-permute-start.15 = (f32[2048,64]{0,1:T(8,128)S(1)}, f32[2048,64]{0,1:T(8,128)S(1)}, u32[]{:S(2)}, u32[]{:S(2)}) collective-permute-start(f32[2048,64]{0,1:T(8,128)S(1)} %add.92), channel_id=1, source_target_pairs={{0,2},{1,3},{2,0},{3,1},{4,6},{5,7},{6,4},{7,5},{8,10},{9,11},{10,... | collective-permute-start | bytes 1572872 | tf_op jit(solution)/shard_map/ppermute | solution.py:43
Sparse Core Ops, SparseCore 0:
  40.1 79.8 all-reduce.8
  158.4 77.9 all-reduce.10
  274.8 77.8 all-reduce.12
  393.1 77.9 all-reduce.14
  512.9 77.8 all-reduce.16
  632.9 77.9 all-reduce.18
  753.2 77.9 all-reduce.20
  873.5 77.8 all-reduce.22
